TPU v7x, 32 devices: a whole 2x2x4 slice. The times are simulated.
32 devices in a mesh: row: 8 (over z, core), loop: 4 (over y, x).
Axes of the slice: x: 2, y: 2, z: 4, core: 2. Of those that a mesh axis runs over, the one named last changes fastest.
Arguments:
- student_image: bfloat16 [5120, 1024], P(('row', 'loop')), may hold values from -12 to 12
- student_text: bfloat16 [5120, 1024], P(('row', 'loop')), may hold values from -12 to 12
- teacher_image: bfloat16 [5120, 1024], P('row', 'loop'), may hold values from -12 to 12
- teacher_text: bfloat16 [5120, 1024], P('row', 'loop'), may hold values from -12 to 12
- student_scale: float32 [1], replicated, may hold values from 30 to 100
- teacher_scale: float32 [1], replicated, may hold values from 30 to 100
Outputs:
- loss: float32 [1], replicated
- grad_image: bfloat16 [5120, 1024], P(('row', 'loop'))
- grad_text: bfloat16 [5120, 1024], P(('row', 'loop'))
All inputs are finite; a program needn't handle non-finite values.
Results may differ from a plain program's by a relative error of at most 0.014.
The roundings to bfloat16 on the way count: a program that leaves them out, or rounds other values in their place, can miss the bound.
Values may be sent and summed in bfloat16 or wider, within the bound.
A program may use at most 128 MiB of HBM per device.

v0:
```python
import jax
import jax.numpy as jnp
from jax import lax
from jax.sharding import PartitionSpec as P

EPS = 1e-06


def unit_rows(codes):
    values = codes.astype(jnp.float32)
    norms = jnp.sqrt(jnp.sum(values * values, axis=1, keepdims=True) + EPS)
    return (values / norms, norms)


def back_norm(grad_unit, units, norms):
    inner = jnp.sum(grad_unit * units, axis=1, keepdims=True)
    return ((grad_unit - units * inner) / norms).astype(jnp.bfloat16)


def on_device(
    student_image, student_text, teacher_image, teacher_text, student_scale, teacher_scale
):
    simg_unit, simg_norm = unit_rows(student_image)
    stxt_unit, stxt_norm = unit_rows(student_text)
    simg_own = simg_unit.astype(jnp.bfloat16)
    stxt_own = stxt_unit.astype(jnp.bfloat16)
    timg_full = lax.all_gather(teacher_image, "loop", axis=1, tiled=True)
    timg = unit_rows(timg_full)[0].astype(jnp.bfloat16)
    ttxt_full = lax.all_to_all(teacher_text, "loop", split_axis=0, concat_axis=1, tiled=True)
    ttxt_own = unit_rows(ttxt_full)[0].astype(jnp.bfloat16)
    simg = lax.all_gather(simg_own, "loop", axis=0, tiled=True)
    stxt, ttxt = (
        lax.all_gather(stxt_own, "row", axis=0, tiled=True),
        lax.all_gather(ttxt_own, "row", axis=0, tiled=True),
    )
    sscale = student_scale[0]
    tscale = teacher_scale[0]
    slog = sscale * jnp.einsum("re,ce->rc", simg, stxt, preferred_element_type=jnp.float32)
    tlog = tscale * jnp.einsum("re,ce->rc", timg, ttxt, preferred_element_type=jnp.float32)
    smax, tmax = lax.pmax((jnp.max(slog, axis=1), jnp.max(tlog, axis=1)), "loop")
    sexp = jnp.exp(slog - smax[:, None])
    texp = jnp.exp(tlog - tmax[:, None])
    ssum, tsum, cross = lax.psum(
        (jnp.sum(sexp, axis=1), jnp.sum(texp, axis=1), jnp.sum(texp * (tlog - slog), axis=1)),
        "loop",
    )
    lses = smax + jnp.log(ssum)
    lset = tmax + jnp.log(tsum)
    diverge = cross / tsum - lset + lses
    group_total = lax.psum(jnp.sum(diverge), "row")
    batch_total = simg.shape[0] * lax.axis_size("row")
    loss = (group_total / batch_total).reshape(1)
    probs = jnp.exp(slog - lses[:, None])
    probt = jnp.exp(tlog - lset[:, None])
    grad_logits = (sscale * (probs - probt)).astype(jnp.bfloat16)
    dimg = lax.psum_scatter(
        jnp.dot(grad_logits, stxt, preferred_element_type=jnp.float32).astype(jnp.bfloat16),
        "loop",
        scatter_dimension=0,
        tiled=True,
    ).astype(jnp.float32)
    dtxt = lax.psum_scatter(
        jnp.einsum("rc,re->ce", grad_logits, simg, preferred_element_type=jnp.float32).astype(
            jnp.bfloat16
        ),
        "row",
        scatter_dimension=0,
        tiled=True,
    ).astype(jnp.float32)
    return (loss, back_norm(dimg, simg_unit, simg_norm), back_norm(dtxt, stxt_unit, stxt_norm))


def solution(mesh):
    return jax.shard_map(
        on_device,
        mesh=mesh,
        in_specs=(
            P(("row", "loop"), None),
            P(("row", "loop"), None),
            P("row", "loop"),
            P("row", "loop"),
            P(),
            P(),
        ),
        out_specs=(P(), P(("row", "loop"), None), P(("row", "loop"), None)),
        check_vma=False,
    )
```

profile of v0, /device:TPU:0, one launch (start us, length us, event | category | flops | bytes accessed | tf_op | source)
XLA Modules:
  0.0 265.1 jit_solution(4238910627074843657)
XLA Ops:
  9.1 1.8 fusion.14
  12.1 1.8 fusion.15
  14.0 14.7 %all_to_all.13 = bf16[4,160,256]{2,1,0:T(8,128)(2,1)S(1)} all-to-all(bf16[4,160,256]{2,1,0:T(8,128)(2,1)S(1)} %bitcast.19), channel_id=1, replica_groups=mesh['row'=8,'loop'=4] {'loop'}, dimensions={0} | all-to-all | bytes 655360 | tf_op jit(solution)/shard_map/all_to_all | solution.py:29
  31.2 12.3 %all-gather.5.cloned.1.call-done = bf16[640,1024]{1,0:T(8,128)(2,1)} async-done(((bf16[640,256]{1,0:T(8,128)(2,1)}), bf16[640,1024]{1,0:T(8,128)(2,1)}) %all-gather.5.cloned.1.call-update) | async-done | bytes 1310736 | tf_op jit(solution)/shard_map/all_gather | solution.py:27
  43.5 1.6 fusion.1
  45.2 29.5 %all-gather.9.cloned.1.call-done = bf16[640,1024]{1,0:T(8,128)(2,1)} async-done(((bf16[160,1024]{1,0:T(8,128)(2,1)}), bf16[640,1024]{1,0:T(8,128)(2,1)}) %all-gather.9.cloned.1.call-update) | async-done | bytes 1310736 | tf_op jit(solution)/shard_map/all_gather | solution.py:31
  74.6 35.4 %all-gather.11.cloned.1.call-done = bf16[1280,1024]{1,0:T(8,128)(2,1)} async-done(((bf16[160,1024]{1,0:T(8,128)(2,1)}), bf16[1280,1024]{1,0:T(8,128)(2,1)}) %all-gather.11.cloned.1.call-update) | async-done | bytes 2621456 | tf_op jit(solution)/shard_map/all_gather | solution.py:33
  110.0 4.2 %fusion.16 = (f32[640]{0:T(1024)S(1)}, f32[640,1280]{1,0:T(8,128)S(1)}) fusion(bf16[640,1024]{1,0:T(8,128)(2,1)} %all-gather.9.cloned.1.call-done, bf16[1280,1024]{1,0:T(8,128)(2,1)} %all-gather.11.cloned.1.call-done, f32[]{:T(128)} %bitcast.15), kind=kOutput, calls=%fused_computation.43 | convolution fusion | flops 1679359360 | bytes 7211524 | tf_op jit(solution)/shard_map/re,ce->rc/dot_general | solution.py:38
  114.2 30.8 %all-gather.7.cloned.1.call-done = bf16[1280,1024]{1,0:T(8,128)(2,1)} async-done(((bf16[160,1024]{1,0:T(8,128)(2,1)}), bf16[1280,1024]{1,0:T(8,128)(2,1)}) %all-gather.7.cloned.1.call-update) | async-done | bytes 2621456 | tf_op jit(solution)/shard_map/all_gather | solution.py:34
  144.9 5.8 %fusion.17 = (f32[640]{0:T(1024)S(1)}, f32[640,1280]{1,0:T(8,128)}) fusion(bf16[1280,1024]{1,0:T(8,128)(2,1)} %all-gather.7.cloned.1.call-done, bf16[640,1024]{1,0:T(8,128)(2,1)} %all-gather.5.cloned.1.call-done, f32[640]{0:T(1024)S(1)} %add_sqrt_fusion, f32[]{:T(128)} %bitcast.17), kind=kOutput, calls=%fused_computation.44 | convolution fusion | flops 1681325440 | bytes 7214084 | tf_op jit(solution)/shard_map/re,ce->rc/dot_general | solution.py:39
  150.7 10.0 %all-reduce.1 = (f32[640]{0:T(1024)S(1)}, f32[640]{0:T(1024)S(1)}) all-reduce(f32[640]{0:T(1024)S(1)} %get-tuple-element.14, f32[640]{0:T(1024)S(1)} %get-tuple-element.16), channel_id=1, replica_groups=mesh['row'=8,'loop'=4] {'loop'}, use_global_device_ids=true, to_apply=%region_11.0 | all-reduce | flops 1280 | bytes 10240 | tf_op jit(solution)/shard_map/pmax | solution.py:40
  160.7 3.3 %multiply_reduce_fusion = (f32[640]{0:T(1024)S(1)}, f32[640]{0:T(1024)S(1)}, f32[640]{0:T(1024)S(1)}) fusion(f32[640,1280]{1,0:T(8,128)} %get-tuple-element.17, f32[640,1280]{1,0:T(8,128)S(1)} %get-tuple-element.15, f32[640]{0:T(1024)S(1)} %get-tuple-element.10, f32[640]{0:T(1024)S(1)} %get-tuple-element.9), kind=kLoop, calls=%fused_computation.5 | loop fusion | flops 5732480 | bytes 6566400 | tf_op jit(solution)/shard_map/reduce_sum | solution.py:44
  164.0 14.0 %all-reduce = (f32[640]{0:T(1024)S(1)}, f32[640]{0:T(1024)S(1)}, f32[640]{0:T(1024)S(1)}) all-reduce(f32[640]{0:T(1024)S(1)} %get-tuple-element.5, f32[640]{0:T(1024)S(1)} %get-tuple-element.4, f32[640]{0:T(1024)S(1)} %get-tuple-element.3), channel_id=1, replica_groups=mesh['row'=8,'loop'=4] {'loop'}, use_global_device_ids=true, to_apply=%region_13.0 | all-reduce | flops 1920 | bytes 15360 | tf_op jit(solution)/shard_map/psum | solution.py:43
  178.7 3.0 %multiply_convert_fusion = bf16[640,1280]{1,0:T(8,128)(2,1)S(1)} fusion(f32[640,1280]{1,0:T(8,128)} %get-tuple-element.17, f32[640,1280]{1,0:T(8,128)S(1)} %get-tuple-element.15, f32[640]{0:T(1024)S(1)} %get-tuple-element.12, f32[640]{0:T(1024)S(1)} %get-tuple-element.13, f32[]{:T(128)} %bitcast.16), kind=kLoop, calls=%fused_computation.3 | loop fusion | flops 4096000 | bytes 8197124 | tf_op jit(solution)/shard_map/convert_element_type | solution.py:55
  181.7 1.2 copy-done.2
  182.9 3.0 %convolution_convert_fusion.1 = bf16[640,1024]{1,0:T(8,128)(2,1)} fusion(bf16[640,1280]{1,0:T(8,128)(2,1)S(1)} %multiply_convert_fusion, bf16[1280,1024]{1,0:T(8,128)(2,1)S(1)} %copy-done.4), kind=kOutput, calls=%fused_computation.12 | convolution fusion | flops 1678376960 | bytes 5570560 | tf_op jit(solution)/shard_map/dot_general | solution.py:57
  186.0 5.2 %convolution_convert_fusion = bf16[1280,1024]{1,0:T(8,128)(2,1)} fusion(bf16[640,1280]{1,0:T(8,128)(2,1)} %copy-done.2, bf16[640,1024]{1,0:T(8,128)(2,1)S(1)} %copy-done.5), kind=kOutput, calls=%fused_computation | convolution fusion | flops 1679032320 | bytes 5570560 | tf_op jit(solution)/shard_map/rc,re->ce/dot_general | solution.py:63
  191.2 14.2 %psum.31 = f32[]{:T(128)} all-reduce(f32[]{:T(128)} %get-tuple-element.11), channel_id=1, replica_groups=mesh['row'=8,'loop'=4] {'row'}, use_global_device_ids=true, to_apply=%region_15.0 | all-reduce | flops 1 | bytes 8 | tf_op jit(solution)/shard_map/psum | solution.py:50
  206.1 7.7 %reduce-scatter.3.cloned.1.call-done = bf16[160,1024]{1,0:T(8,128)(2,1)} async-done(((bf16[640,1024]{1,0:T(8,128)(2,1)}), bf16[160,1024]{1,0:T(8,128)(2,1)}) %reduce-scatter.3.cloned.1.call-update) | async-done | bytes 327696 | tf_op jit(solution)/shard_map/reduce_scatter | solution.py:56
  213.8 1.2 fusion.7
  215.0 2.0 fusion.9
  217.0 37.0 %reduce-scatter.5.cloned.1.call-done = bf16[160,1024]{1,0:T(8,128)(2,1)} async-done(((bf16[1280,1024]{1,0:T(8,128)(2,1)}), bf16[160,1024]{1,0:T(8,128)(2,1)}) %reduce-scatter.5.cloned.1.call-update) | async-done | bytes 327696 | tf_op jit(solution)/shard_map/reduce_scatter | solution.py:62
  253.9 1.2 fusion.10
  255.2 2.0 fusion.12
  (34 shorter events, 5.0 us)
Async XLA Ops:
  7.2 6.9 %copy-start.3 = (bf16[640,256]{1,0:T(8,128)(2,1)S(1)}, bf16[640,256]{1,0:T(8,128)(2,1)}, u32[]{:S(2)}) copy-start(bf16[640,256]{1,0:T(8,128)(2,1)} %param.9) | copy-start | bytes 983044
  7.2 36.3 %all-gather.5.cloned.1.call-start = ((), (), s32[]{:S(2)}) async-start(), calls=%async_computation.3 | async-start | bytes 1638400 | tf_op jit(solution)/shard_map/all_gather | solution.py:27
  7.9 66.7 %all-gather.9.cloned.1.call-start = ((), (), s32[]{:S(2)}) async-start(), calls=%async_computation.5 | async-start | bytes 1638400 | tf_op jit(solution)/shard_map/all_gather | solution.py:31
  10.9 99.1 %all-gather.11.cloned.1.call-start = ((), (), s32[]{:S(2)}) async-start(), calls=%async_computation.6 | async-start | bytes 2949120 | tf_op jit(solution)/shard_map/all_gather | solution.py:33
  14.0 131.0 %all-gather.7.cloned.1.call-start = ((), (), s32[]{:S(2)}) async-start(), calls=%async_computation.4 | async-start | bytes 2949120 | tf_op jit(solution)/shard_map/all_gather | solution.py:34
  29.9 183.9 %reduce-scatter.3.cloned.1.call-start = ((), (), s32[]{:S(2)}) async-start(), calls=%async_computation.7 | async-start | bytes 1638400 | tf_op jit(solution)/shard_map/reduce_scatter | solution.py:56
  178.7 4.2 %copy-start.4 = (bf16[1280,1024]{1,0:T(8,128)(2,1)S(1)}, bf16[1280,1024]{1,0:T(8,128)(2,1)}, u32[]{:S(2)}) copy-start(bf16[1280,1024]{1,0:T(8,128)(2,1)} %all-gather.11.cloned.1.call-done) | copy-start | bytes 7864324
  181.7 1.2 copy-start.2
  182.9 3.1 %copy-start.5 = (bf16[640,1024]{1,0:T(8,128)(2,1)S(1)}, bf16[640,1024]{1,0:T(8,128)(2,1)}, u32[]{:S(2)}) copy-start(bf16[640,1024]{1,0:T(8,128)(2,1)} %all-gather.9.cloned.1.call-done) | copy-start | bytes 3932164
  185.9 68.0 %reduce-scatter.5.cloned.1.call-start = ((), (), s32[]{:S(2)}) async-start(), calls=%async_computation.8 | async-start | bytes 2949120 | tf_op jit(solution)/shard_map/reduce_scatter | solution.py:62
  191.2 22.6 %copy-start = (bf16[160,1024]{1,0:T(8,128)(2,1)S(1)}, bf16[160,1024]{1,0:T(8,128)(2,1)}, u32[]{:S(2)}) copy-start(bf16[160,1024]{1,0:T(8,128)(2,1)} %param.6) | copy-start | bytes 983044
  191.2 62.8 %copy-start.1 = (bf16[160,1024]{1,0:T(8,128)(2,1)S(1)}, bf16[160,1024]{1,0:T(8,128)(2,1)}, u32[]{:S(2)}) copy-start(bf16[160,1024]{1,0:T(8,128)(2,1)} %param.7) | copy-start | bytes 983044
Sparse Core Ops, SparseCore 0:
  9.8 33.6 all-gather.4
  45.9 28.6 all-gather.8
  76.3 33.6 all-gather.10
  112.1 32.8 all-gather.6
  186.0 27.6 reduce-scatter.2
  215.9 37.9 reduce-scatter.4
where the time goes:
time: 266 us; the launch traced here: 265 us
  waiting for transfers between devices  153 us (58%)
  blocking collectives  52.9 us (20%)
  other arithmetic  22 us (8%)
  matrix products  18.1 us (7%)
  between operations  17.3 us (7%)
    reduce_scatter x1, waiting for transfers between devices, on_device(): lax.psum_scatter(jnp.einsum('rc,re->ce', grad_logits, simg, preferred_ele...  37 us
    all_gather x1, waiting for transfers between devices, on_device(): lax.all_gather(stxt_own, 'row', axis=0, tiled=True)  35.4 us
    all_gather x1, waiting for transfers between devices, on_device(): lax.all_gather(ttxt_own, 'row', axis=0, tiled=True)  30.8 us
    all_gather x1, waiting for transfers between devices, on_device(): simg = lax.all_gather(simg_own, 'loop', axis=0, tiled=True)  29.5 us
    all_to_all x1, blocking collectives, on_device(): lax.all_to_all(teacher_text, 'loop', split_axis=0, concat_axis=1, tiled=T...  14.7 us
    psum x1, blocking collectives, on_device(): group_total = lax.psum(jnp.sum(diverge), 'row')  14.2 us
    psum x1, blocking collectives, on_device(): lax.psum((jnp.sum(sexp, axis=1), jnp.sum(texp, axis=1), jnp.sum(texp * (t...  14 us
    all_gather x1, waiting for transfers between devices, on_device(): timg_full = lax.all_gather(teacher_image, 'loop', axis=1, tiled=True)  12.3 us
  transfers between devices with their start and end apart: 6, of which 6 were waited for; matrix products, arithmetic and copies ran while one was open for 8% of the time, Pallas kernels for 0%

commit v1 on v0

--- a/solution.py
+++ b/solution.py
@@ -28,7 +28,12 @@
     timg = unit_rows(timg_full)[0].astype(jnp.bfloat16)
     ttxt_full = lax.all_to_all(teacher_text, "loop", split_axis=0, concat_axis=1, tiled=True)
     ttxt_own = unit_rows(ttxt_full)[0].astype(jnp.bfloat16)
-    simg = lax.all_gather(simg_own, "loop", axis=0, tiled=True)
+    ring = [simg_own]
+    for hop in range(3):
+        ring.append(lax.ppermute(ring[-1], "loop", [(dev, (dev + 1) % 4) for dev in range(4)]))
+    simg = jnp.roll(
+        jnp.concatenate(ring[::-1], axis=0), (lax.axis_index("loop") + 1) * ring[0].shape[0], axis=0
+    )
     stxt, ttxt = (
         lax.all_gather(stxt_own, "row", axis=0, tiled=True),
         lax.all_gather(ttxt_own, "row", axis=0, tiled=True),

time: 266 us -> 239 us (0.90)
  waiting for transfers between devices: 153 us -> 125 us
  local copies, waits for them, and re-layouts: 1.26 us -> 5.85 us
  blocking collectives: 52.9 us -> 50.2 us
    ppermute x0 -> x3, waiting for transfers between devices: none -> 32.2 us  [on_device(): lax.ppermute(ring[-1], 'loop', [(dev, (dev + 1) % 4) for dev in range(4)])]
    all_gather x1 -> x0, waiting for transfers between devices: 29.5 us -> none  [on_device(): simg = lax.all_gather(simg_own, 'loop', axis=0, tiled=True)]
    all_gather x1, waiting for transfers between devices: 35.4 us -> 16.9 us  [on_device(): lax.all_gather(stxt_own, 'row', axis=0, tiled=True)]
    all_gather x1, waiting for transfers between devices: 12.3 us -> 0.01 us  [on_device(): timg_full = lax.all_gather(teacher_image, 'loop', axis=1, tiled=True)]
    unnamed x12 -> x16, local copies, waits for them, and re-layouts: 1.2 us -> 5.78 us
    all_to_all x1, blocking collectives: 14.7 us -> 11.9 us  [on_device(): lax.all_to_all(teacher_text, 'loop', split_axis=0, concat_axis=1, tiled=T...]
  transfers between devices with their start and end apart: 6 -> 8, of which waited for: 6 -> 7; matrix products, arithmetic and copies ran while one was open for 8% -> 11% of each run, Pallas kernels for 0% -> 0%
where the time goes in v1:
time: 239 us; the launch traced here: 238 us
  waiting for transfers between devices  125 us (52%)
  blocking collectives  50.2 us (21%)
  other arithmetic  21 us (9%)
  matrix products  18.5 us (8%)
  between operations  16.9 us (7%)
  local copies, waits for them, and re-layouts  5.85 us (2%)
    reduce_scatter x1, waiting for transfers between devices, on_device(): lax.psum_scatter(jnp.einsum('rc,re->ce', grad_logits, simg, preferred_ele...  36.8 us
    ppermute x3, waiting for transfers between devices, on_device(): lax.ppermute(ring[-1], 'loop', [(dev, (dev + 1) % 4) for dev in range(4)])  32.2 us
    all_gather x1, waiting for transfers between devices, on_device(): lax.all_gather(ttxt_own, 'row', axis=0, tiled=True)  30.9 us
    all_gather x1, waiting for transfers between devices, on_device(): lax.all_gather(stxt_own, 'row', axis=0, tiled=True)  16.9 us
    psum x1, blocking collectives, on_device(): group_total = lax.psum(jnp.sum(diverge), 'row')  14.2 us
    psum x1, blocking collectives, on_device(): lax.psum((jnp.sum(sexp, axis=1), jnp.sum(texp, axis=1), jnp.sum(texp * (t...  14 us
    all_to_all x1, blocking collectives, on_device(): lax.all_to_all(teacher_text, 'loop', split_axis=0, concat_axis=1, tiled=T...  11.9 us
    pmax x1, blocking collectives, on_device(): lax.pmax((jnp.max(slog, axis=1), jnp.max(tlog, axis=1)), 'loop')  9.97 us
  transfers between devices with their start and end apart: 8, of which 7 were waited for; matrix products, arithmetic and copies ran while one was open for 11% of the time, Pallas kernels for 0%

profile of v1, /device:TPU:0, one launch (start us, length us, event | category | flops | bytes accessed | tf_op | source)
XLA Modules:
  0.0 238.3 jit_solution(4907904773538077246)
XLA Ops:
  9.1 1.8 fusion.19
  11.0 11.9 %all_to_all.13 = bf16[4,160,256]{2,1,0:T(8,128)(2,1)S(1)} all-to-all(bf16[4,160,256]{2,1,0:T(8,128)(2,1)} %bitcast.17), channel_id=1, replica_groups=mesh['row'=8,'loop'=4] {'loop'}, dimensions={0} | all-to-all | bytes 655360 | tf_op jit(solution)/shard_map/all_to_all | solution.py:29
  25.2 8.8 %collective-permute-done = bf16[160,1024]{1,0:T(8,128)(2,1)S(1)} collective-permute-done((bf16[160,1024]{1,0:T(8,128)(2,1)S(1)}, bf16[160,1024]{1,0:T(8,128)(2,1)S(1)}, u32[]{:S(2)}, u32[]{:S(2)}) %collective-permute-start) | collective-permute-done | bytes 327712 | tf_op jit(solution)/shard_map/ppermute | solution.py:33
  34.1 15.0 %collective-permute-done.1 = bf16[160,1024]{1,0:T(8,128)(2,1)S(1)} collective-permute-done((bf16[160,1024]{1,0:T(8,128)(2,1)S(1)}, bf16[160,1024]{1,0:T(8,128)(2,1)S(1)}, u32[]{:S(2)}, u32[]{:S(2)}) %collective-permute-start.1) | collective-permute-done | bytes 327712 | tf_op jit(solution)/shard_map/ppermute | solution.py:33
  50.4 8.3 %collective-permute-done.2 = bf16[160,1024]{1,0:T(8,128)(2,1)S(1)} collective-permute-done((bf16[160,1024]{1,0:T(8,128)(2,1)S(1)}, bf16[160,1024]{1,0:T(8,128)(2,1)S(1)}, u32[]{:S(2)}, u32[]{:S(2)}) %collective-permute-start.2) | collective-permute-done | bytes 327712 | tf_op jit(solution)/shard_map/ppermute | solution.py:33
  65.0 1.6 fusion.1
  66.7 16.9 %all-gather.8.cloned.1.call-done = bf16[1280,1024]{1,0:T(8,128)(2,1)} async-done(((bf16[160,1024]{1,0:T(8,128)(2,1)}), bf16[1280,1024]{1,0:T(8,128)(2,1)}) %all-gather.8.cloned.1.call-update) | async-done | bytes 2621456 | tf_op jit(solution)/shard_map/all_gather | solution.py:38
  83.5 4.2 %fusion.20 = (f32[640]{0:T(1024)S(1)}, f32[640,1280]{1,0:T(8,128)S(1)}) fusion(bf16[1280,1024]{1,0:T(8,128)(2,1)} %all-gather.8.cloned.1.call-done, bf16[1280,1024]{1,0:T(8,128)(2,1)} %constant_dynamic-update-slice_fusion, s32[]{:T(128)S(6)} %select_n.14, f32[]{:T(128)} %bitcast.13), kind=kOutput, calls=%fused_computation.55 | convolution fusion | flops 1679359360 | bytes 7212036 | tf_op jit(solution)/shard_map/re,ce->rc/dot_general | solution.py:43
  87.7 30.9 %all-gather.6.cloned.1.call-done = bf16[1280,1024]{1,0:T(8,128)(2,1)} async-done(((bf16[160,1024]{1,0:T(8,128)(2,1)}), bf16[1280,1024]{1,0:T(8,128)(2,1)}) %all-gather.6.cloned.1.call-update) | async-done | bytes 2621456 | tf_op jit(solution)/shard_map/all_gather | solution.py:39
  118.6 5.8 %fusion.21 = (f32[640]{0:T(1024)S(1)}, f32[640,1280]{1,0:T(8,128)}) fusion(bf16[1280,1024]{1,0:T(8,128)(2,1)} %all-gather.6.cloned.1.call-done, bf16[640,1024]{1,0:T(8,128)(2,1)} %all-gather.4.cloned.1.call-done, f32[640]{0:T(1024)S(1)} %add_sqrt_fusion, f32[]{:T(128)} %bitcast.15), kind=kOutput, calls=%fused_computation.56 | convolution fusion | flops 1681325440 | bytes 7214084 | tf_op jit(solution)/shard_map/re,ce->rc/dot_general | solution.py:44
  124.4 10.0 %all-reduce.1 = (f32[640]{0:T(1024)S(1)}, f32[640]{0:T(1024)S(1)}) all-reduce(f32[640]{0:T(1024)S(1)} %get-tuple-element.14, f32[640]{0:T(1024)S(1)} %get-tuple-element.16), channel_id=1, replica_groups=mesh['row'=8,'loop'=4] {'loop'}, use_global_device_ids=true, to_apply=%region_11.12 | all-reduce | flops 1280 | bytes 10240 | tf_op jit(solution)/shard_map/pmax | solution.py:45
  134.4 3.3 %multiply_reduce_fusion = (f32[640]{0:T(1024)S(1)}, f32[640]{0:T(1024)S(1)}, f32[640]{0:T(1024)S(1)}) fusion(f32[640,1280]{1,0:T(8,128)} %get-tuple-element.17, f32[640,1280]{1,0:T(8,128)S(1)} %get-tuple-element.15, f32[640]{0:T(1024)S(1)} %get-tuple-element.10, f32[640]{0:T(1024)S(1)} %get-tuple-element.9), kind=kLoop, calls=%fused_computation.5 | loop fusion | flops 5732480 | bytes 6566400 | tf_op jit(solution)/shard_map/reduce_sum | solution.py:49
  137.7 14.0 %all-reduce = (f32[640]{0:T(1024)S(1)}, f32[640]{0:T(1024)S(1)}, f32[640]{0:T(1024)S(1)}) all-reduce(f32[640]{0:T(1024)S(1)} %get-tuple-element.5, f32[640]{0:T(1024)S(1)} %get-tuple-element.4, f32[640]{0:T(1024)S(1)} %get-tuple-element.3), channel_id=1, replica_groups=mesh['row'=8,'loop'=4] {'loop'}, use_global_device_ids=true, to_apply=%region_13.14 | all-reduce | flops 1920 | bytes 15360 | tf_op jit(solution)/shard_map/psum | solution.py:48
  152.3 3.0 %multiply_convert_fusion = bf16[640,1280]{1,0:T(8,128)(2,1)S(1)} fusion(f32[640,1280]{1,0:T(8,128)} %get-tuple-element.17, f32[640,1280]{1,0:T(8,128)S(1)} %get-tuple-element.15, f32[640]{0:T(1024)S(1)} %get-tuple-element.12, f32[640]{0:T(1024)S(1)} %get-tuple-element.13, f32[]{:T(128)} %bitcast.14), kind=kLoop, calls=%fused_computation.3 | loop fusion | flops 4096000 | bytes 8197124 | tf_op jit(solution)/shard_map/convert_element_type | solution.py:60
  155.4 1.2 copy-done.3
  156.6 3.0 %convolution_convert_fusion.1 = bf16[640,1024]{1,0:T(8,128)(2,1)} fusion(bf16[640,1280]{1,0:T(8,128)(2,1)S(1)} %multiply_convert_fusion, bf16[1280,1024]{1,0:T(8,128)(2,1)S(1)} %copy-done.4), kind=kOutput, calls=%fused_computation.12 | convolution fusion | flops 1678376960 | bytes 5570560 | tf_op jit(solution)/shard_map/dot_general | solution.py:62
  159.6 5.6 %convolution_convert_fusion = bf16[1280,1024]{1,0:T(8,128)(2,1)} fusion(bf16[640,1280]{1,0:T(8,128)(2,1)} %copy-done.3, bf16[1280,1024]{1,0:T(8,128)(2,1)} %constant_dynamic-update-slice_fusion, s32[]{:T(128)S(6)} %select_n.14), kind=kOutput, calls=%fused_computation | convolution fusion | flops 1679032320 | bytes 5570564 | tf_op jit(solution)/shard_map/rc,re->ce/dot_general | solution.py:68
  165.2 14.2 %psum.31 = f32[]{:T(128)} all-reduce(f32[]{:T(128)} %get-tuple-element.11), channel_id=1, replica_groups=mesh['row'=8,'loop'=4] {'row'}, use_global_device_ids=true, to_apply=%region_15.16 | all-reduce | flops 1 | bytes 8 | tf_op jit(solution)/shard_map/psum | solution.py:55
  180.1 7.3 %reduce-scatter.3.cloned.1.call-done = bf16[160,1024]{1,0:T(8,128)(2,1)} async-done(((bf16[640,1024]{1,0:T(8,128)(2,1)}), bf16[160,1024]{1,0:T(8,128)(2,1)}) %reduce-scatter.3.cloned.1.call-update) | async-done | bytes 327696 | tf_op jit(solution)/shard_map/reduce_scatter | solution.py:61
  187.4 1.2 fusion.9
  188.7 2.0 fusion.11
  190.6 36.8 %reduce-scatter.5.cloned.1.call-done = bf16[160,1024]{1,0:T(8,128)(2,1)} async-done(((bf16[1280,1024]{1,0:T(8,128)(2,1)}), bf16[160,1024]{1,0:T(8,128)(2,1)}) %reduce-scatter.5.cloned.1.call-update) | async-done | bytes 327696 | tf_op jit(solution)/shard_map/reduce_scatter | solution.py:67
  227.4 1.2 fusion.12
  228.7 2.0 fusion.14
  (43 shorter events, 11.2 us)
Async XLA Ops:
  7.2 57.8 %all-gather.4.cloned.1.call-start = ((), (), s32[]{:S(2)}) async-start(), calls=%async_computation.3 | async-start | bytes 1638400 | tf_op jit(solution)/shard_map/all_gather | solution.py:27
  7.9 75.6 %all-gather.8.cloned.1.call-start = ((), (), s32[]{:S(2)}) async-start(), calls=%async_computation.5 | async-start | bytes 2949120 | tf_op jit(solution)/shard_map/all_gather | solution.py:38
  10.9 13.2 %copy-start = (bf16[160,1024]{1,0:T(8,128)(2,1)S(1)}, bf16[160,1024]{1,0:T(8,128)(2,1)}, u32[]{:S(2)}) copy-start(bf16[160,1024]{1,0:T(8,128)(2,1)} %param.6) | copy-start | bytes 983044
  10.9 107.7 %all-gather.6.cloned.1.call-start = ((), (), s32[]{:S(2)}) async-start(), calls=%async_computation.4 | async-start | bytes 2949120 | tf_op jit(solution)/shard_map/all_gather | solution.py:39
  24.1 163.4 %reduce-scatter.3.cloned.1.call-start = ((), (), s32[]{:S(2)}) async-start(), calls=%async_computation.6 | async-start | bytes 1638400 | tf_op jit(solution)/shard_map/reduce_scatter | solution.py:61
  24.4 9.6 %collective-permute-start = (bf16[160,1024]{1,0:T(8,128)(2,1)S(1)}, bf16[160,1024]{1,0:T(8,128)(2,1)S(1)}, u32[]{:S(2)}, u32[]{:S(2)}) collective-permute-start(bf16[160,1024]{1,0:T(8,128)(2,1)S(1)} %fusion.18), channel_id=1, source_target_pairs={{0,1},{1,2},{2,3},{3,0},{4,5},{5,6},{6,7},{7,4},{8,9},{9,10},{10,1... | collective-permute-start | bytes 983048 | tf_op jit(solution)/shard_map/ppermute | solution.py:33
  34.1 15.0 %collective-permute-start.1 = (bf16[160,1024]{1,0:T(8,128)(2,1)S(1)}, bf16[160,1024]{1,0:T(8,128)(2,1)S(1)}, u32[]{:S(2)}, u32[]{:S(2)}) collective-permute-start(bf16[160,1024]{1,0:T(8,128)(2,1)S(1)} %collective-permute-done), channel_id=1, source_target_pairs={{0,1},{1,2},{2,3},{3,0},{4,5},{5,6},{6,7},{7,4},{8,9},{9,10},{10,1... | collective-permute-start | bytes 983048 | tf_op jit(solution)/shard_map/ppermute | solution.py:33
  49.1 9.6 %collective-permute-start.2 = (bf16[160,1024]{1,0:T(8,128)(2,1)S(1)}, bf16[160,1024]{1,0:T(8,128)(2,1)S(1)}, u32[]{:S(2)}, u32[]{:S(2)}) collective-permute-start(bf16[160,1024]{1,0:T(8,128)(2,1)S(1)} %collective-permute-done.1), channel_id=1, source_target_pairs={{0,1},{1,2},{2,3},{3,0},{4,5},{5,6},{6,7},{7,4},{8,9},{9,10},{10,1... | collective-permute-start | bytes 983048 | tf_op jit(solution)/shard_map/ppermute | solution.py:33
  152.3 4.2 %copy-start.4 = (bf16[1280,1024]{1,0:T(8,128)(2,1)S(1)}, bf16[1280,1024]{1,0:T(8,128)(2,1)}, u32[]{:S(2)}) copy-start(bf16[1280,1024]{1,0:T(8,128)(2,1)} %all-gather.8.cloned.1.call-done) | copy-start | bytes 7864324
  155.4 1.2 copy-start.3
  159.6 67.9 %reduce-scatter.5.cloned.1.call-start = ((), (), s32[]{:S(2)}) async-start(), calls=%async_computation.7 | async-start | bytes 2949120 | tf_op jit(solution)/shard_map/reduce_scatter | solution.py:67
  165.2 22.2 %copy-start.1 = (bf16[160,1024]{1,0:T(8,128)(2,1)S(1)}, bf16[160,1024]{1,0:T(8,128)(2,1)}, u32[]{:S(2)}) copy-start(bf16[160,1024]{1,0:T(8,128)(2,1)} %param.6) | copy-start | bytes 983044
  165.2 62.2 %copy-start.2 = (bf16[160,1024]{1,0:T(8,128)(2,1)S(1)}, bf16[160,1024]{1,0:T(8,128)(2,1)}, u32[]{:S(2)}) copy-start(bf16[160,1024]{1,0:T(8,128)(2,1)} %param.7) | copy-start | bytes 983044
Sparse Core Ops, SparseCore 0:
  9.8 37.4 all-gather.3
  49.5 33.9 all-gather.7
  85.7 32.8 all-gather.5
  159.7 27.6 reduce-scatter.2
  189.6 37.8 reduce-scatter.4
